TPU v7x, 512 devices: a whole 4x8x8 slice. The times are simulated.
512 devices in a mesh: seq: 32 (over y_hi, x, core), head: 16 (over z, y_lo).
Axes of the slice: x: 4, y: 8 (y_hi: 4, y_lo: 2; y = y_hi * 2 + y_lo), z: 8, core: 2. Of those that a mesh axis runs over, the one named last changes fastest.
Arguments:
- queries: bfloat16 [12288, 32, 128], P(('seq', 'head')), may hold values from -8 to 8
- keys: bfloat16 [12288, 16, 128], P(('seq', 'head')), may hold values from -8 to 8
- values: bfloat16 [12288, 16, 128], P(('seq', 'head')), may hold values from -6 to 6
- output_gradient: bfloat16 [12288, 32, 128], P(('seq', 'head')), may hold values from -6 to 6
- doc_lengths: int32 [8], replicated, may hold values from 1 to 9216, 12288 in all
Outputs:
- query_grad: bfloat16 [12288, 32, 128], P(('seq', 'head'))
- key_grad: bfloat16 [12288, 16, 128], P(('seq', 'head'))
- value_grad: bfloat16 [12288, 16, 128], P(('seq', 'head'))
Inputs may be any that keep to these rules, and one draw needn't show every extreme that they name: `doc_lengths`: the lengths sum to 12288; the longest has exactly 9216 tokens.
All inputs are finite; a program needn't handle non-finite values.
Results may differ from a plain program's by a relative error of at most 0.02.
Values may be sent and summed in bfloat16 or wider, within the bound.
A program may use at most 64 MiB of HBM per device.

v0:
```python
import math

import jax
import jax.numpy as jnp
from jax import lax
from jax.experimental import pallas as pl
from jax.experimental.pallas import tpu as pltpu
from jax.sharding import PartitionSpec as P

WINDOW = 4096

score_scale = 144.0 ** (-0.5)
exp2_scale = score_scale * math.log2(math.e)
masked_value = -1e30


def attention_kernel(
    base_ref, lo_ref, pos_ref, x_ref, kv_hbm, dq_ref, dkv_ref, kv_ref, s_ref, dp_ref, sem
):
    rows = x_ref.shape[0]
    tiles, _, wide = s_ref.shape
    dim = kv_ref.shape[1] // 2
    base = pl.multiple_of(base_ref[0], rows)
    copy = pltpu.make_async_copy(kv_hbm.at[pl.ds(base, tiles * rows), :], kv_ref, sem)
    copy.start()
    q = jnp.concatenate([x_ref[:, :dim], x_ref[:, dim : 2 * dim]], axis=0)
    g = jnp.concatenate([x_ref[:, 2 * dim : 3 * dim], x_ref[:, 3 * dim : 4 * dim]], axis=0)
    lo = lo_ref[...]
    pos = pos_ref[...]
    copy.wait()

    def first(t, top):
        k_tile = kv_ref[pl.ds(pl.multiple_of(t * rows, rows), rows), :dim]
        s = lax.dot_general(k_tile, q, (((1,), (1,)), ((), ())), preferred_element_type=jnp.float32)
        k_pos = base + t * rows + lax.broadcasted_iota(jnp.int32, (rows, wide), 0)
        s = jnp.where((k_pos >= lo) & (k_pos <= pos), s, masked_value)
        s_ref[t] = s
        return jnp.maximum(top, jnp.max(s, axis=0, keepdims=True))

    top = lax.fori_loop(0, tiles, first, jnp.full((1, wide), masked_value, jnp.float32))
    top = top * exp2_scale

    def second(t, state):
        total, delta = state
        v_tile = kv_ref[pl.ds(pl.multiple_of(t * rows, rows), rows), dim:]
        dp = lax.dot_general(
            v_tile, g, (((1,), (1,)), ((), ())), preferred_element_type=jnp.float32
        )
        p = jnp.exp2(s_ref[t] * exp2_scale - top)
        s_ref[t] = p
        dp_ref[t] = dp
        return (
            total + jnp.sum(p, axis=0, keepdims=True),
            delta + jnp.sum(p * dp, axis=0, keepdims=True),
        )

    zero = jnp.zeros((1, wide), jnp.float32)
    total, delta = lax.fori_loop(0, tiles, second, (zero, zero))
    inverse = 1.0 / total
    delta = delta * inverse
    column = jnp.transpose(jnp.broadcast_to(inverse, (dim, wide)))
    g_low = (g.astype(jnp.float32) * column).astype(jnp.bfloat16)
    q_low = (q.astype(jnp.float32) * (column * score_scale)).astype(jnp.bfloat16)

    def third(t, dq):
        at = pl.ds(pl.multiple_of(t * rows, rows), rows)
        p = s_ref[t]
        ds = (p * (dp_ref[t] - delta)).astype(jnp.bfloat16)
        dv = jnp.dot(p.astype(jnp.bfloat16), g_low, preferred_element_type=jnp.float32)
        dk = jnp.dot(ds, q_low, preferred_element_type=jnp.float32)
        dkv_ref[at, :dim] = dk.astype(jnp.bfloat16)
        dkv_ref[at, dim:] = dv.astype(jnp.bfloat16)
        return dq + lax.dot_general(
            kv_ref[at, :dim], ds, (((0,), (0,)), ((), ())), preferred_element_type=jnp.float32
        )

    dq = lax.fori_loop(0, tiles, third, jnp.zeros((dim, wide), jnp.float32))
    dq = jnp.transpose(dq * (inverse * score_scale)).astype(jnp.bfloat16)
    dq_ref[:, :dim] = dq[:rows]
    dq_ref[:, dim:] = dq[rows:]


def body(queries, keys, values, output_gradient, doc_lengths):
    chunk, kv_heads, dim = keys.shape
    group = queries.shape[1] // kv_heads
    seq_count = lax.axis_size("seq")
    my_index = lax.axis_index("seq")
    packed = jnp.concatenate(
        [
            queries.reshape(chunk, kv_heads, group * dim),
            output_gradient.reshape(chunk, kv_heads, group * dim),
            keys,
            values,
        ],
        axis=2,
    )
    local = lax.all_to_all(packed, "head", split_axis=1, concat_axis=0, tiled=True)
    rows = local.shape[0]
    local = local.reshape(rows, local.shape[2])
    kv_all = lax.all_gather(local[:, 2 * group * dim :], "seq", axis=0, tiled=True)
    reach = min((WINDOW - 1) // rows + 1, seq_count - 1)
    tiles = reach + 1
    base = jnp.clip(my_index - reach, 0, seq_count - tiles) * rows
    pos = my_index * rows + jnp.arange(rows, dtype=jnp.int32)
    ends = jnp.cumsum(doc_lengths)
    doc_start = jnp.max(jnp.where(ends[None, :] <= pos[:, None], ends[None, :], 0), axis=1)
    lo = jnp.maximum(doc_start, pos - (WINDOW - 1))
    wide = group * rows
    lo = jnp.tile(lo, group).reshape(1, wide).astype(jnp.int32)
    pos = jnp.tile(pos, group).reshape(1, wide)
    vmem = pl.BlockSpec(memory_space=pltpu.VMEM)
    dq, dkv = pl.pallas_call(
        attention_kernel,
        out_shape=(
            jax.ShapeDtypeStruct((rows, group * dim), jnp.bfloat16),
            jax.ShapeDtypeStruct((tiles * rows, 2 * dim), jnp.bfloat16),
        ),
        in_specs=[
            pl.BlockSpec(memory_space=pltpu.SMEM),
            vmem,
            vmem,
            vmem,
            pl.BlockSpec(memory_space=pl.ANY),
        ],
        out_specs=(vmem, vmem),
        scratch_shapes=[
            pltpu.VMEM((tiles * rows, 2 * dim), jnp.bfloat16),
            pltpu.VMEM((tiles, rows, wide), jnp.float32),
            pltpu.VMEM((tiles, rows, wide), jnp.float32),
            pltpu.SemaphoreType.DMA,
        ],
        compiler_params=pltpu.CompilerParams(vmem_limit_bytes=60 * 2**20),
        name="attention_backward",
    )(base.reshape(1).astype(jnp.int32), lo, pos, local[:, : 2 * group * dim], kv_all)
    spread = jnp.zeros((seq_count * rows, 2 * dim), jnp.bfloat16)
    spread = lax.dynamic_update_slice_in_dim(spread, dkv, base, axis=0)
    own = lax.psum_scatter(spread, "seq", scatter_dimension=0, tiled=True)
    back = jnp.concatenate([dq, own], axis=1).reshape(rows, 1, (group + 2) * dim)
    back = lax.all_to_all(back, "head", split_axis=0, concat_axis=1, tiled=True)
    return (
        back[:, :, : group * dim].reshape(queries.shape),
        back[:, :, group * dim : (group + 1) * dim],
        back[:, :, (group + 1) * dim :],
    )


def solution(mesh):
    spec = P(("seq", "head"), None, None)
    return jax.shard_map(
        body,
        mesh=mesh,
        in_specs=(spec, spec, spec, spec, P()),
        out_specs=(spec, spec, spec),
        check_vma=False,
    )
```

profile of v0, /device:TPU:6, one launch (start us, length us, event | category | flops | bytes accessed | tf_op | source)
XLA Modules:
  0.0 285.9 jit_solution(3645103770940328308)
XLA Ops:
  7.2 0.0 all-gather.2.cloned.1.call-start
  7.2 1.0 reshape.66
  8.2 0.0 copy-start.2
  8.2 0.1 copy.34
  8.3 1.0 reshape.67
  9.3 0.1 copy.35
  9.4 0.9 copy.36
  10.3 0.9 copy.37
  11.2 0.1 pad_maximum_fusion
  11.3 29.9 %all_to_all.33 = bf16[24,16,768]{2,0,1:T(8,128)(2,1)S(1)} all-to-all(bf16[24,16,768]{2,0,1:T(8,128)(2,1)S(1)} %pad_maximum_fusion), channel_id=1, replica_groups=mesh['seq'=32,'head'=16] {'head'}, dimensions={1} | all-to-all | bytes 1179648 | tf_op jit(solution)/shard_map/all_to_all | solution.py:97
  41.2 0.7 slice.21
  41.9 0.0 all-gather.2.cloned.1.call-update
  41.9 0.0 reduce-scatter.2.cloned.1.call-start
  41.9 0.0 copy-done.2
  42.0 0.2 reduce-window.8
  42.1 0.1 select_reduce_fusion
  42.2 0.6 copy.43
  42.8 0.6 copy.44
  43.4 0.8 slice.20.x_ref
  44.2 67.5 %all-gather.2.cloned.1.call-done.kv_hbm = bf16[12288,256]{1,0:T(8,128)(2,1)} async-done(((bf16[384,256]{1,0:T(8,128)(2,1)}), bf16[12288,256]{1,0:T(8,128)(2,1)}) %all-gather.2.cloned.1.call-update) | async-done | bytes 6291472 | tf_op jit(solution)/shard_map/all_gather | solution.py:100
  111.7 20.7 %attention_backward.1 = (bf16[384,256]{1,0:T(8,128)(2,1)}, bf16[4608,256]{1,0:T(8,128)(2,1)}) custom-call(s32[1]{0:T(128)} %bitcast.base_ref, s32[1,768]{1,0:T(1,128)} %bitcast.27, s32[1,768]{1,0:T(1,128)} %bitcast.28, bf16[384,512]{1,0:T(8,128)(2,1)} %slice.20.x_ref, bf16[12288,256]{1,0:T(8,128)(2,1)} %all-gather.2.cloned.1.call-done.kv_hbm), custom_call_target="tpu_custom_call" | custom-call | tf_op jit(solution)/shard_map/attention_backward/pallas_call | solution.py:112
  132.5 0.0 copy-start
  132.5 3.0 %broadcast_in_dim.17 = bf16[12288,256]{1,0:T(8,128)(2,1)} broadcast(bf16[]{:T(256)} %constant.25.clone.1), dimensions={} | broadcast | bytes 6291458 | tf_op jit(solution)/shard_map/broadcast_in_dim | solution.py:135
  135.4 0.0 copy-done
  135.5 1.6 constant_dynamic-update-slice_fusion
  137.1 0.0 copy-start.1
  137.1 0.0 reduce-scatter.2.cloned.1.call-update
  137.1 115.8 %reduce-scatter.2.cloned.1.call-done = bf16[384,256]{1,0:T(8,128)(2,1)} async-done(((bf16[12288,256]{1,0:T(8,128)(2,1)}), bf16[384,256]{1,0:T(8,128)(2,1)}) %reduce-scatter.2.cloned.1.call-update) | async-done | bytes 196624 | tf_op jit(solution)/shard_map/reduce_scatter | solution.py:137
  252.9 0.0 copy-done.1
  252.9 1.0 maximum_bitcast_fusion
  253.9 0.5 broadcast.20
  254.4 0.9 reduce
  255.3 0.1 reshape.71
  255.5 20.9 %all_to_all.34 = bf16[16,2,6144]{2,1,0:T(2,128)(2,1)S(1)} all-to-all(bf16[16,2,6144]{2,1,0:T(2,128)(2,1)S(1)} %reshape.71), channel_id=1, replica_groups=mesh['seq'=32,'head'=16] {'head'}, dimensions={0} | all-to-all | bytes 786432 | tf_op jit(solution)/shard_map/all_to_all | solution.py:139
  276.4 0.4 reshape.72
  276.8 0.1 copy.42
  276.9 0.7 copy.40
  277.6 0.7 copy.41
  278.3 0.7 reshape.70
  (7 shorter events, 0.1 us)
Async XLA Ops:
  7.2 104.6 %all-gather.2.cloned.1.call-start = ((), (), s32[]{:S(2)}) async-start(), calls=%async_computation.3 | async-start | bytes 6488064 | tf_op jit(solution)/shard_map/all_gather | solution.py:100
  8.2 33.7 %copy-start.2 = (s32[8]{0:T(128)S(1)}, s32[8]{0:T(128)}, u32[]{:S(2)}) copy-start(s32[8]{0:T(128)} %param.9) | copy-start | bytes 100
  41.9 211.0 %reduce-scatter.2.cloned.1.call-start = ((), (), s32[]{:S(2)}) async-start(), calls=%async_computation.4 | async-start | bytes 6488064 | tf_op jit(solution)/shard_map/reduce_scatter | solution.py:137
  132.5 3.0 %copy-start = (bf16[4608,256]{1,0:T(8,128)(2,1)S(1)}, bf16[4608,256]{1,0:T(8,128)(2,1)}, u32[]{:S(2)}) copy-start(bf16[4608,256]{1,0:T(8,128)(2,1)} %get-tuple-element.6) | copy-start | bytes 7077892
  137.1 115.9 %copy-start.1 = (bf16[384,256]{1,0:T(8,128)(2,1)S(1)}, bf16[384,256]{1,0:T(8,128)(2,1)}, u32[]{:S(2)}) copy-start(bf16[384,256]{1,0:T(8,128)(2,1)} %get-tuple-element.5) | copy-start | bytes 589828
Sparse Core Ops, SparseCore 0:
  42.0 69.6 all-gather.1
  137.2 115.6 reduce-scatter.1
where the time goes:
time: 287 us; the launch traced here: 286 us
  waiting for transfers between devices  183 us (64%)
  blocking collectives  50.8 us (18%)
  Pallas kernels  20.7 us (7%)
  local copies, waits for them, and re-layouts  14.4 us (5%)
  between operations  14.2 us (5%)
    reduce_scatter x1, waiting for transfers between devices, body(): own = lax.psum_scatter(spread, 'seq', scatter_dimension=0, tiled=True)  116 us
    all_gather x1, waiting for transfers between devices, body(): lax.all_gather(local[:, 2 * group * dim:], 'seq', axis=0, tiled=True)  67.5 us
    all_to_all x1, blocking collectives, body(): lax.all_to_all(packed, 'head', split_axis=1, concat_axis=0, tiled=True)  29.9 us
    all_to_all x1, blocking collectives, body(): back = lax.all_to_all(back, 'head', split_axis=0, concat_axis=1, tiled=True)  20.9 us
    pallas_call x1, Pallas kernels, body(): pl.pallas_call(attention_kernel, out_shape=(jax.ShapeDtypeStruct((rows, g...  20.7 us
  transfers between devices with their start and end apart: 2, of which 2 were waited for; matrix products, arithmetic and copies ran while one was open for 1% of the time, Pallas kernels for 0%

commit v1 on v0

v1 whole, which is shorter than its diff:
```python
import math

import jax
import jax.numpy as jnp
from jax import lax
from jax.experimental import pallas as pl
from jax.experimental.pallas import tpu as pltpu
from jax.sharding import PartitionSpec as P

WINDOW = 4096

score_scale = 144.0 ** (-0.5)
exp2_scale = score_scale * math.log2(math.e)
masked_value = -1e30


def attention_kernel(
    lo_ref, pos_ref, x_ref, out_ref,
    kv_ref, s_ref, dp_ref, dq_ref, odd_ref, even_ref, pair_ref, got_ref, row_ref,
    partner_send, across_send, chip_send, slot_recv, odd_send, even_send, pair_recv, row_send, got_recv,
):
    rows = x_ref.shape[0]
    reach, _, wide = s_ref.shape
    dim = kv_ref.shape[2] // 2
    my = lax.axis_index("seq")
    my_head = lax.axis_index("head")
    grid_rows = lax.axis_size("seq") // 8
    row = my // 8
    chip = my // 2 - row * 4
    core = my - (my // 2) * 2
    order = my // 2

    def place(r, x, c):
        return (r * 8 + x * 2 + c, my_head)

    def remote(source, target, send, recv, device):
        return pltpu.make_async_remote_copy(
            src_ref=source,
            dst_ref=target,
            send_sem=send,
            recv_sem=recv,
            device_id=device,
            device_id_type=pl.DeviceIdType.MESH,
        )

    def slot_copy(source, target, send, device):
        return remote(kv_ref.at[source], kv_ref.at[target], send, slot_recv.at[target], device)

    def arrived(slot):
        slot_copy(slot, slot, chip_send.at[0], place(row, chip, core)).wait_recv()

    def got(index):
        remote(
            got_ref.at[index],
            got_ref.at[index],
            row_send.at[0],
            got_recv.at[index],
            place(row, chip, core),
        ).wait_recv()

    extra = 13
    has_next = row < grid_rows - 1
    relays = chip >= 3 - core

    def to_next(act):
        @pl.when(has_next)
        def _():
            act(slot_copy(0, 8, across_send.at[0], place(row + 1, chip, core)))

    def to_second(act):
        @pl.when((row >= 1) & has_next & relays)
        def _():
            act(slot_copy(8, extra, across_send.at[1], place(row + 1, chip, core)))

    def along_own(act):
        for other in range(4):
            @pl.when(chip < other)
            def _(other=other):
                act(
                    slot_copy(
                        0, 2 * (other - chip), chip_send.at[other], place(row, other, core)
                    )
                )

    def along_first(act):
        for other in range(4):
            @pl.when((row >= 1) & (chip != other) & (chip + 1 + core >= other))
            def _(other=other):
                act(
                    slot_copy(
                        8, 8 + 2 * (other - chip), chip_send.at[4 + other], place(row, other, core)
                    )
                )

    def along_second(act):
        for other in range(2):
            @pl.when((row >= 2) & (chip - 3 + core >= other))
            def _(other=other):
                act(
                    slot_copy(
                        extra,
                        16 + 2 * (other - chip),
                        chip_send.at[8 + other],
                        place(row, other, core),
                    )
                )

    def to_partner(j, act):
        @pl.when(core == 0)
        def _():
            act(slot_copy(2 * j, 2 * j + 1, partner_send.at[j], place(row, chip, 1)))

        @pl.when((core == 1) & (j >= 1))
        def _():
            act(slot_copy(2 * j, 2 * j - 1, partner_send.at[j], place(row, chip, 0)))

    def start(copy):
        copy.start()

    def sent(copy):
        copy.wait_send()

    kv_ref[0] = x_ref[:, 4 * dim :]

    barrier = pltpu.get_barrier_semaphore()

    def greet(device):
        pl.semaphore_signal(
            barrier, inc=1, device_id=device, device_id_type=pl.DeviceIdType.MESH
        )

    for step in range(1, 4):
        greet(place(row, (chip + step) % 4, core))
    greet(place(row, chip, 1 - core))

    greet(place((row + 1) % grid_rows, chip, core))
    greet(place((row + grid_rows - 1) % grid_rows, chip, core))
    pl.semaphore_wait(barrier, 6)

    to_next(start)
    along_own(start)
    to_partner(0, start)

    q = jnp.concatenate([x_ref[:, :dim], x_ref[:, dim : 2 * dim]], axis=0)
    g = jnp.concatenate([x_ref[:, 2 * dim : 3 * dim], x_ref[:, 3 * dim : 4 * dim]], axis=0)
    lo = lo_ref[...]
    pos = pos_ref[...]

    def scores(d, top):
        contract = (((1,), (1,)), ((), ()))
        s = lax.dot_general(kv_ref[d, :, :dim], q, contract, preferred_element_type=jnp.float32)
        dp_ref[d] = lax.dot_general(
            kv_ref[d, :, dim:], g, contract, preferred_element_type=jnp.float32
        )
        k_pos = (my - d) * rows + lax.broadcasted_iota(jnp.int32, (rows, wide), 0)
        s = jnp.where((k_pos >= lo) & (k_pos <= pos), s, masked_value)
        s_ref[d] = s
        return jnp.maximum(top, jnp.max(s, axis=0, keepdims=True))

    top = scores(0, jnp.full((1, wide), masked_value, jnp.float32))

    @pl.when(row >= 1)
    def _():
        arrived(8)

    to_second(start)
    along_first(start)

    def even_step(j, top):
        @pl.when(j != 4)
        def _():
            arrived(2 * j)

        to_partner(j, start)
        return scores(2 * j, top)

    even_end = jnp.minimum(order, 5) + 1
    top = lax.fori_loop(1, jnp.minimum(even_end, 3), even_step, top)

    @pl.when((row >= 2) & relays)
    def _():
        arrived(extra)

    along_second(start)
    top = lax.fori_loop(3, even_end, even_step, top)
    last = (core == 1) & (order >= 6)

    @pl.when(last)
    def _():
        arrived(12)
        slot_copy(12, 11, partner_send.at[6], place(row, chip, 0)).start()

    def odd_step(j, top):
        arrived(2 * j + 1)
        return scores(2 * j + 1, top)

    top = lax.fori_loop(0, jnp.minimum(order + core, 6), odd_step, top)
    top = top * exp2_scale

    def second(d, state):
        total, delta = state
        p = jnp.exp2(s_ref[d] * exp2_scale - top)
        s_ref[d] = p
        return (
            total + jnp.sum(p, axis=0, keepdims=True),
            delta + jnp.sum(p * dp_ref[d], axis=0, keepdims=True),
        )

    zero = jnp.zeros((1, wide), jnp.float32)
    total, delta = lax.fori_loop(0, jnp.minimum(my + 1, reach), second, (zero, zero))
    inverse = 1.0 / total
    delta = delta * inverse
    column = jnp.transpose(jnp.broadcast_to(inverse, (dim, wide)))
    g_low = (g.astype(jnp.float32) * column).astype(jnp.bfloat16)
    q_low = (q.astype(jnp.float32) * (column * score_scale)).astype(jnp.bfloat16)
    dq_ref[...] = jnp.zeros_like(dq_ref)

    def gradients(d):
        p = s_ref[d]
        ds = (p * (dp_ref[d] - delta)).astype(jnp.bfloat16)
        dv = jnp.dot(p.astype(jnp.bfloat16), g_low, preferred_element_type=jnp.float32)
        dk = jnp.dot(ds, q_low, preferred_element_type=jnp.float32)
        dq_ref[...] += lax.dot_general(
            kv_ref[d, :, :dim], ds, (((0,), (0,)), ((), ())), preferred_element_type=jnp.float32
        )
        return dk, dv

    def odd_copy(j):
        return remote(
            odd_ref.at[j],
            pair_ref.at[j],
            odd_send.at[j],
            pair_recv.at[j],
            place(row, chip, 1 - core),
        )

    def dispatch(k, act):
        @pl.when((k >= 1) & (k <= chip))
        def _():
            act(
                remote(
                    even_ref.at[k],
                    got_ref.at[k],
                    even_send.at[k],
                    got_recv.at[k],
                    place(row, chip - k, core),
                )
            )

        @pl.when((k > chip) & (k <= chip + 4) & (k != 4))
        def _():
            act(
                remote(
                    even_ref.at[k],
                    got_ref.at[4 + chip],
                    even_send.at[k],
                    got_recv.at[4 + chip],
                    place(row, chip - k + 4, core),
                )
            )

        @pl.when(k > chip + 4)
        def _():
            act(
                remote(
                    even_ref.at[k],
                    got_ref.at[8 + chip],
                    even_send.at[k],
                    got_recv.at[8 + chip],
                    place(row, chip - k + 8, core),
                )
            )

    def third(i, carry):
        j = jnp.minimum(order, 5) - i
        sends = (core == 1) | (j < order)
        gets = (core == 0) | (j < order)

        @pl.when(sends)
        def _():
            dk, dv = gradients(2 * j + 1)
            odd_ref[j, :, :dim] = dk.astype(jnp.bfloat16)
            odd_ref[j, :, dim:] = dv.astype(jnp.bfloat16)
            odd_copy(j).start()

        @pl.when(gets & (j + core <= 5))
        def _():
            dk, dv = gradients(2 * (j + core))
            odd_copy(j).wait_recv()
            even_ref[j + core, :, :dim] = (
                dk + pair_ref[j, :, :dim].astype(jnp.float32)
            ).astype(jnp.bfloat16)
            even_ref[j + core, :, dim:] = (
                dv + pair_ref[j, :, dim:].astype(jnp.float32)
            ).astype(jnp.bfloat16)
            dispatch(j + core, start)

        @pl.when(gets & (j + core == 6))
        def _():
            odd_copy(j).wait_recv()
            even_ref[6] = pair_ref[j]
            dispatch(6, start)

        return carry

    lax.fori_loop(0, jnp.minimum(order, 5) + 1, third, 0)

    @pl.when(core == 1)
    def _():
        dk, dv = gradients(0)
        even_ref[0, :, :dim] = dk.astype(jnp.bfloat16)
        even_ref[0, :, dim:] = dv.astype(jnp.bfloat16)

    dq = jnp.transpose(dq_ref[...] * (inverse * score_scale)).astype(jnp.bfloat16)
    out_ref[:, :dim] = dq[:rows]
    out_ref[:, dim : 2 * dim] = dq[rows:]

    acc = dp_ref.at[0, :, : 2 * dim]

    def add(index):
        got(index)
        acc[...] += got_ref[index].astype(jnp.float32)

    def row_copy(index):
        return remote(
            row_ref.at[index],
            got_ref.at[10 + index],
            row_send.at[index],
            got_recv.at[10 + index],
            place(row - 1, chip, core),
        )

    @pl.when((row >= 2) & relays)
    def _():
        acc[...] = jnp.zeros((rows, 2 * dim), jnp.float32)
        for other in range(2):
            @pl.when(chip - 3 + core >= other)
            def _(other=other):
                add(8 + other)

        row_ref[1] = acc[...].astype(jnp.bfloat16)
        row_copy(1).start()

    @pl.when(row >= 1)
    def _():
        acc[...] = even_ref[4].astype(jnp.float32)
        for other in range(4):
            @pl.when((chip != other) & (chip + 1 + core >= other))
            def _(other=other):
                add(4 + other)

        @pl.when(has_next & relays)
        def _():
            add(11)

        row_ref[0] = acc[...].astype(jnp.bfloat16)
        row_copy(0).start()

    acc[...] = even_ref[0].astype(jnp.float32)
    for k in range(1, 4):
        @pl.when(chip + k <= 3)
        def _(k=k):
            add(k)

    @pl.when(has_next)
    def _():
        add(10)

    out_ref[:, 2 * dim :] = acc[...].astype(jnp.bfloat16)

    to_next(sent)
    along_own(sent)
    to_second(sent)
    along_first(sent)
    along_second(sent)

    def sent_pair(j, carry):
        to_partner(j, sent)
        return carry

    lax.fori_loop(0, even_end, sent_pair, 0)

    @pl.when(last)
    def _():
        slot_copy(12, 11, partner_send.at[6], place(row, chip, 0)).wait_send()

    def sent_gradients(j, carry):
        @pl.when((core == 1) | (j < order))
        def _():
            odd_copy(j).wait_send()

        @pl.when((core == 0) | (j < order))
        def _():
            dispatch(j + core, sent)

        return carry

    lax.fori_loop(0, even_end, sent_gradients, 0)

    @pl.when((row >= 2) & relays)
    def _():
        row_copy(1).wait_send()

    @pl.when(row >= 1)
    def _():
        row_copy(0).wait_send()


def body(queries, keys, values, output_gradient, doc_lengths):
    chunk, kv_heads, dim = keys.shape
    group = queries.shape[1] // kv_heads
    seq_count = lax.axis_size("seq")
    my_index = lax.axis_index("seq")
    packed = jnp.concatenate(
        [
            queries.reshape(chunk, kv_heads, group * dim),
            output_gradient.reshape(chunk, kv_heads, group * dim),
            keys,
            values,
        ],
        axis=2,
    )
    local = lax.all_to_all(packed, "head", split_axis=1, concat_axis=0, tiled=True)
    rows = local.shape[0]
    local = local.reshape(rows, local.shape[2])
    reach = (WINDOW - 1) // rows + 2
    pos = my_index * rows + jnp.arange(rows, dtype=jnp.int32)
    ends = jnp.cumsum(doc_lengths)
    doc_start = jnp.max(jnp.where(ends[None, :] <= pos[:, None], ends[None, :], 0), axis=1)
    lo = jnp.maximum(doc_start, pos - (WINDOW - 1))
    wide = group * rows
    lo = jnp.tile(lo, group).reshape(1, wide).astype(jnp.int32)
    pos = jnp.tile(pos, group).reshape(1, wide)
    vmem = pl.BlockSpec(memory_space=pltpu.VMEM)
    block = (rows, 2 * dim)
    dma = pltpu.SemaphoreType.DMA
    back = pl.pallas_call(
        attention_kernel,
        out_shape=jax.ShapeDtypeStruct((rows, (group + 2) * dim), jnp.bfloat16),
        in_specs=[vmem, vmem, vmem],
        out_specs=vmem,
        scratch_shapes=[
            pltpu.VMEM((14,) + block, jnp.bfloat16),
            pltpu.VMEM((reach, rows, wide), jnp.float32),
            pltpu.VMEM((reach, rows, wide), jnp.float32),
            pltpu.VMEM((dim, wide), jnp.float32),
            pltpu.VMEM((6,) + block, jnp.bfloat16),
            pltpu.VMEM((7,) + block, jnp.bfloat16),
            pltpu.VMEM((6,) + block, jnp.bfloat16),
            pltpu.VMEM((12,) + block, jnp.bfloat16),
            pltpu.VMEM((2,) + block, jnp.bfloat16),
            dma((7,)),
            dma((2,)),
            dma((10,)),
            dma((14,)),
            dma((6,)),
            dma((7,)),
            dma((6,)),
            dma((2,)),
            dma((12,)),
        ],
        compiler_params=pltpu.CompilerParams(
            vmem_limit_bytes=60 * 2**20, collective_id=0, has_side_effects=True
        ),
        name="attention_backward",
    )(lo, pos, local)
    back = back.reshape(rows, 1, (group + 2) * dim)
    back = lax.all_to_all(back, "head", split_axis=0, concat_axis=1, tiled=True)
    return (
        back[:, :, : group * dim].reshape(queries.shape),
        back[:, :, group * dim : (group + 1) * dim],
        back[:, :, (group + 1) * dim :],
    )


def solution(mesh):
    spec = P(("seq", "head"), None, None)
    return jax.shard_map(
        body,
        mesh=mesh,
        in_specs=(spec, spec, spec, spec, P()),
        out_specs=(spec, spec, spec),
        check_vma=False,
    )
```

time: 287 us -> 128 us (0.45)
  waiting for transfers between devices: 183 us -> 16.9 us
  Pallas kernels: 20.7 us -> 65.9 us
  blocking collectives: 50.8 us -> 22.7 us
  between operations: 14.2 us -> 0.8 us
  starting transfers between devices: 0.08 us -> 11.6 us
  local copies, waits for them, and re-layouts: 14.4 us -> 6.52 us
    reduce_scatter x1 -> x0, waiting for transfers between devices: 116 us -> none  [body(): own = lax.psum_scatter(spread, 'seq', scatter_dimension=0, tiled=True)]
    all_gather x1 -> x0, waiting for transfers between devices: 67.5 us -> none  [body(): lax.all_gather(local[:, 2 * group * dim:], 'seq', axis=0, tiled=True)]
    pallas_call x1, Pallas kernels: 20.7 us -> 65.9 us  [body(): pl.pallas_call(attention_kernel, out_shape=jax.ShapeDtypeStruct((rows, (g...]
    all_to_all x1 -> x0, blocking collectives: 29.9 us -> none  [body(): lax.all_to_all(packed, 'head', split_axis=1, concat_axis=0, tiled=True)]
    all_to_all x0 -> x1, waiting for transfers between devices: none -> 16.9 us  [body(): lax.all_to_all(packed, 'head', split_axis=1, concat_axis=0, tiled=True)]
    all_to_all x0 -> x1, starting transfers between devices: none -> 11.6 us  [body(): lax.all_to_all(packed, 'head', split_axis=1, concat_axis=0, tiled=True)]
    broadcast_in_dim x1 -> x0, local copies, waits for them, and re-layouts: 2.96 us -> none  [body(): spread = jnp.zeros((seq_count * rows, 2 * dim), jnp.bfloat16)]
  transfers between devices with their start and end apart: 2 -> 1, of which waited for: 2 -> 1; matrix products, arithmetic and copies ran while one was open for 1% -> 1% of each run, Pallas kernels for 0% -> 0%
where the time goes in v1:
time: 128 us; the launch traced here: 127 us
  Pallas kernels  65.9 us (51%)
  blocking collectives  22.7 us (18%)
  waiting for transfers between devices  16.9 us (13%)
  starting transfers between devices  11.6 us (9%)
  local copies, waits for them, and re-layouts  6.52 us (5%)
  other arithmetic  3.03 us (2%)
    pallas_call x1, Pallas kernels, body(): pl.pallas_call(attention_kernel, out_shape=jax.ShapeDtypeStruct((rows, (g...  65.9 us
    all_to_all x1, blocking collectives, body(): back = lax.all_to_all(back, 'head', split_axis=0, concat_axis=1, tiled=True)  22.7 us
    all_to_all x1, waiting for transfers between devices, body(): lax.all_to_all(packed, 'head', split_axis=1, concat_axis=0, tiled=True)  16.9 us
    all_to_all x1, starting transfers between devices, body(): lax.all_to_all(packed, 'head', split_axis=1, concat_axis=0, tiled=True)  11.6 us
    unnamed x21, local copies, waits for them, and re-layouts  3.94 us
  transfers between devices with their start and end apart: 1, of which 1 were waited for; matrix products, arithmetic and copies ran while one was open for 1% of the time, Pallas kernels for 0%

profile of v1, /device:TPU:6, one launch (start us, length us, event | category | flops | bytes accessed | tf_op | source)
XLA Modules:
  0.0 127.4 jit_solution(13036998370860471333)
XLA Ops:
  0.6 0.0 copy-start.1
  0.6 0.0 copy-start.2
  0.7 0.0 copy-start.3
  0.7 1.0 reshape.62
  1.7 0.1 copy.34
  1.8 0.0 copy-done.1
  1.8 0.1 reshape.63
  1.9 0.1 copy.35
  1.9 0.0 copy-done.2
  2.0 0.0 copy-done.3
  2.0 0.9 pad_maximum_fusion
  2.9 0.0 copy-start.4
  2.9 11.6 %all-to-all-start = ((bf16[24,16,768]{2,0,1:T(8,128)(2,1)}), bf16[24,16,768]{2,0,1:T(8,128)(2,1)S(1)}, u32[]{:S(2)}, u32[]{:S(2)}) async-start(bf16[24,16,768]{2,0,1:T(8,128)(2,1)} %pad_maximum_fusion), calls=%async_computation | async-start | bytes 1179648 | tf_op jit(solution)/shard_map/all_to_all | solution.py:423
  14.5 0.0 copy-done.4
  14.5 0.2 reduce-window.8
  14.7 0.1 select_reduce_fusion
  14.8 0.6 copy.43
  15.3 0.6 copy.44
  15.9 16.9 %all-to-all-done = bf16[24,16,768]{2,0,1:T(8,128)(2,1)S(1)} async-done(((bf16[24,16,768]{2,0,1:T(8,128)(2,1)}), bf16[24,16,768]{2,0,1:T(8,128)(2,1)S(1)}, u32[]{:S(2)}, u32[]{:S(2)}) %all-to-all-start) | async-done | bytes 589856 | tf_op jit(solution)/shard_map/all_to_all | solution.py:423
  32.8 0.0 copy-start
  32.8 0.8 copy-done
  33.6 65.9 %attention_backward.1 = bf16[384,512]{1,0:T(8,128)(2,1)} custom-call(s32[1,768]{1,0:T(1,128)} %bitcast.25, s32[1,768]{1,0:T(1,128)} %bitcast.26, bf16[384,768]{1,0:T(8,128)(2,1)} %bitcast.21), custom_call_target="tpu_custom_call" | custom-call | tf_op jit(solution)/shard_map/attention_backward/pallas_call | solution.py:437
  99.5 0.5 broadcast.20
  100.0 1.9 %reduce = bf16[384,512]{1,0:T(8,128)(2,1)S(1)} reduce(bf16[384,1,512]{2,0,1:T(8,128)(2,1)} %bitcast.24, bf16[]{:T(256)} %broadcast.20), dimensions={1}, to_apply=%copy.38.reduce_sub_computation | reduce | bytes 786434 | tf_op jit(solution)/shard_map/reshape | solution.py:467
  101.9 0.1 reshape.67
  102.1 22.7 %all_to_all.33 = bf16[16,2,6144]{2,1,0:T(2,128)(2,1)S(1)} all-to-all(bf16[16,2,6144]{2,1,0:T(2,128)(2,1)S(1)} %reshape.67), channel_id=1, replica_groups=mesh['seq'=32,'head'=16] {'head'}, dimensions={0} | all-to-all | bytes 786432 | tf_op jit(solution)/shard_map/all_to_all | solution.py:468
  124.8 0.4 reshape.68
  125.2 0.1 copy.42
  125.3 0.7 copy.40
  126.0 0.7 copy.41
  126.7 0.7 reshape.66
  (9 shorter events, 0.2 us)
Async XLA Ops:
  0.6 1.1 copy-start.1
  0.6 1.3 %copy-start.2 = (bf16[24,16,128]{2,1,0:T(8,128)(2,1)S(1)}, bf16[24,16,128]{2,1,0:T(8,128)(2,1)}, u32[]{:S(2)}) copy-start(bf16[24,16,128]{2,1,0:T(8,128)(2,1)} %param.6) | copy-start | bytes 294916
  0.7 1.3 %copy-start.3 = (bf16[24,16,128]{2,1,0:T(8,128)(2,1)S(1)}, bf16[24,16,128]{2,1,0:T(8,128)(2,1)}, u32[]{:S(2)}) copy-start(bf16[24,16,128]{2,1,0:T(8,128)(2,1)} %param.7) | copy-start | bytes 294916
  2.9 11.6 %copy-start.4 = (s32[8]{0:T(128)S(1)}, s32[8]{0:T(128)}, u32[]{:S(2)}) copy-start(s32[8]{0:T(128)} %param.9) | copy-start | bytes 100
  2.9 29.9 %all-to-all-start = ((bf16[24,16,768]{2,0,1:T(8,128)(2,1)}), bf16[24,16,768]{2,0,1:T(8,128)(2,1)S(1)}, u32[]{:S(2)}, u32[]{:S(2)}) async-start(bf16[24,16,768]{2,0,1:T(8,128)(2,1)} %pad_maximum_fusion), calls=%async_computation | async-start | bytes 1179648 | tf_op jit(solution)/shard_map/all_to_all | solution.py:423
  32.8 0.8 copy-start

commit v2 on v1

--- a/solution.py
+++ b/solution.py
@@ -15,11 +15,13 @@
 
 
 def attention_kernel(
-    lo_ref, pos_ref, x_ref, out_ref,
-    kv_ref, s_ref, dp_ref, dq_ref, odd_ref, even_ref, pair_ref, got_ref, row_ref,
+    lengths_ref, kv_out_ref, qg_out_ref, dq_back_ref, dkv_back_ref,
+    kv_in_ref, qg_in_ref, dq_out_ref, dkv_out_ref, kv_ref, s_ref, dp_ref, dq_ref, odd_ref, even_ref, pair_ref, got_ref, row_ref,
     partner_send, across_send, chip_send, slot_recv, odd_send, even_send, pair_recv, row_send, got_recv,
+    swap_send, swap_recv,
 ):
-    rows = x_ref.shape[0]
+    heads, chunk, _ = kv_out_ref.shape
+    rows = heads * chunk
     reach, _, wide = s_ref.shape
     dim = kv_ref.shape[2] // 2
     my = lax.axis_index("seq")
@@ -120,7 +122,43 @@
     def sent(copy):
         copy.wait_send()
 
-    kv_ref[0] = x_ref[:, 4 * dim :]
+    def swap(n, source, target, peer):
+        return remote(
+            source.at[peer],
+            target.at[my_head],
+            swap_send.at[n * heads + peer],
+            swap_recv.at[n * heads + my_head],
+            (my, peer),
+        )
+
+    def swap_start(n, source, target):
+        def one(step, carry):
+            swap(n, source, target, (my_head + step) % heads).start()
+            return carry
+
+        lax.fori_loop(1, heads, one, 0)
+        target[my_head] = source[my_head]
+
+    def swap_arrived(n, source, target):
+        def one(step, carry):
+            peer = (my_head + step) % heads
+            remote(
+                source.at[peer],
+                target.at[peer],
+                swap_send.at[n * heads + peer],
+                swap_recv.at[n * heads + peer],
+                (my, peer),
+            ).wait_recv()
+            return carry
+
+        lax.fori_loop(1, heads, one, 0)
+
+    def swap_sent(n, source, target):
+        def one(step, carry):
+            swap(n, source, target, (my_head + step) % heads).wait_send()
+            return carry
+
+        lax.fori_loop(1, heads, one, 0)
 
     barrier = pltpu.get_barrier_semaphore()
 
@@ -135,16 +173,35 @@
 
     greet(place((row + 1) % grid_rows, chip, core))
     greet(place((row + grid_rows - 1) % grid_rows, chip, core))
-    pl.semaphore_wait(barrier, 6)
+
+    def greet_head(step, carry):
+        greet((my, (my_head + step) % heads))
+        return carry
+
+    lax.fori_loop(1, heads, greet_head, 0)
+    pl.semaphore_wait(barrier, 5 + heads)
+    swap_start(0, kv_out_ref, kv_in_ref)
+    swap_start(1, qg_out_ref, qg_in_ref)
+    swap_arrived(0, kv_out_ref, kv_in_ref)
+    kv_ref[0] = kv_in_ref[...].astype(jnp.float32).reshape(rows, 2 * dim).astype(jnp.bfloat16)
 
     to_next(start)
     along_own(start)
     to_partner(0, start)
 
-    q = jnp.concatenate([x_ref[:, :dim], x_ref[:, dim : 2 * dim]], axis=0)
-    g = jnp.concatenate([x_ref[:, 2 * dim : 3 * dim], x_ref[:, 3 * dim : 4 * dim]], axis=0)
-    lo = lo_ref[...]
-    pos = pos_ref[...]
+    pos = my * rows + lax.broadcasted_iota(jnp.int32, (1, rows), 1)
+    end = lengths_ref[0]
+    lo = jnp.zeros((1, rows), jnp.int32)
+    for document in range(1, lengths_ref.shape[0]):
+        lo = jnp.where(pos >= end, end, lo)
+        end = end + lengths_ref[document]
+    lo = jnp.maximum(lo, pos - (WINDOW - 1))
+    pos = jnp.concatenate([pos] * (wide // rows), axis=1)
+    lo = jnp.concatenate([lo] * (wide // rows), axis=1)
+    swap_arrived(1, qg_out_ref, qg_in_ref)
+    qg = qg_in_ref[...].astype(jnp.float32).reshape(rows, 4 * dim).astype(jnp.bfloat16)
+    q = jnp.concatenate([qg[:, :dim], qg[:, dim : 2 * dim]], axis=0)
+    g = jnp.concatenate([qg[:, 2 * dim : 3 * dim], qg[:, 3 * dim :]], axis=0)
 
     def scores(d, top):
         contract = (((1,), (1,)), ((), ()))
@@ -311,9 +368,12 @@
         even_ref[0, :, :dim] = dk.astype(jnp.bfloat16)
         even_ref[0, :, dim:] = dv.astype(jnp.bfloat16)
 
-    dq = jnp.transpose(dq_ref[...] * (inverse * score_scale)).astype(jnp.bfloat16)
-    out_ref[:, :dim] = dq[:rows]
-    out_ref[:, dim : 2 * dim] = dq[rows:]
+    dq = jnp.transpose(dq_ref[...] * (inverse * score_scale))
+    for part in range(2):
+        dq_out_ref[:, :, part * dim : (part + 1) * dim] = (
+            dq[part * rows : (part + 1) * rows].reshape(heads, chunk, dim).astype(jnp.bfloat16)
+        )
+    swap_start(2, dq_out_ref, dq_back_ref)
 
     acc = dp_ref.at[0, :, : 2 * dim]
 
@@ -366,7 +426,8 @@
     def _():
         add(10)
 
-    out_ref[:, 2 * dim :] = acc[...].astype(jnp.bfloat16)
+    dkv_out_ref[...] = acc[...].reshape(heads, chunk, 2 * dim).astype(jnp.bfloat16)
+    swap_start(3, dkv_out_ref, dkv_back_ref)
 
     to_next(sent)
     along_own(sent)
@@ -405,50 +466,52 @@
     def _():
         row_copy(0).wait_send()
 
+    swap_sent(0, kv_out_ref, kv_in_ref)
+    swap_sent(1, qg_out_ref, qg_in_ref)
+    swap_sent(2, dq_out_ref, dq_back_ref)
+    swap_sent(3, dkv_out_ref, dkv_back_ref)
+    swap_arrived(2, dq_out_ref, dq_back_ref)
+    swap_arrived(3, dkv_out_ref, dkv_back_ref)
+
 
 def body(queries, keys, values, output_gradient, doc_lengths):
     chunk, kv_heads, dim = keys.shape
     group = queries.shape[1] // kv_heads
-    seq_count = lax.axis_size("seq")
-    my_index = lax.axis_index("seq")
-    packed = jnp.concatenate(
-        [
-            queries.reshape(chunk, kv_heads, group * dim),
-            output_gradient.reshape(chunk, kv_heads, group * dim),
-            keys,
-            values,
-        ],
-        axis=2,
+    rows = chunk * lax.axis_size("head")
+    by_head = lambda parts: jnp.transpose(
+        jnp.concatenate([part.reshape(chunk, kv_heads, -1) for part in parts], axis=2), (1, 0, 2)
     )
-    local = lax.all_to_all(packed, "head", split_axis=1, concat_axis=0, tiled=True)
-    rows = local.shape[0]
-    local = local.reshape(rows, local.shape[2])
+    kv = by_head([keys, values])
+    qg = by_head([queries, output_gradient])
     reach = (WINDOW - 1) // rows + 2
-    pos = my_index * rows + jnp.arange(rows, dtype=jnp.int32)
-    ends = jnp.cumsum(doc_lengths)
-    doc_start = jnp.max(jnp.where(ends[None, :] <= pos[:, None], ends[None, :], 0), axis=1)
-    lo = jnp.maximum(doc_start, pos - (WINDOW - 1))
     wide = group * rows
-    lo = jnp.tile(lo, group).reshape(1, wide).astype(jnp.int32)
-    pos = jnp.tile(pos, group).reshape(1, wide)
     vmem = pl.BlockSpec(memory_space=pltpu.VMEM)
     block = (rows, 2 * dim)
+    swapped = (kv_heads, chunk, 2 * dim)
+    low = jnp.bfloat16
     dma = pltpu.SemaphoreType.DMA
-    back = pl.pallas_call(
+    dq, dkv = pl.pallas_call(
         attention_kernel,
-        out_shape=jax.ShapeDtypeStruct((rows, (group + 2) * dim), jnp.bfloat16),
-        in_specs=[vmem, vmem, vmem],
-        out_specs=vmem,
+        out_shape=(
+            jax.ShapeDtypeStruct(swapped, low),
+            jax.ShapeDtypeStruct(swapped, low),
+        ),
+        in_specs=[pl.BlockSpec(memory_space=pltpu.SMEM), vmem, vmem],
+        out_specs=(vmem, vmem),
         scratch_shapes=[
-            pltpu.VMEM((14,) + block, jnp.bfloat16),
+            pltpu.VMEM(swapped, low),
+            pltpu.VMEM((kv_heads, chunk, 4 * dim), low),
+            pltpu.VMEM(swapped, low),
+            pltpu.VMEM(swapped, low),
+            pltpu.VMEM((14,) + block, low),
             pltpu.VMEM((reach, rows, wide), jnp.float32),
             pltpu.VMEM((reach, rows, wide), jnp.float32),
             pltpu.VMEM((dim, wide), jnp.float32),
-            pltpu.VMEM((6,) + block, jnp.bfloat16),
-            pltpu.VMEM((7,) + block, jnp.bfloat16),
-            pltpu.VMEM((6,) + block, jnp.bfloat16),
-            pltpu.VMEM((12,) + block, jnp.bfloat16),
-            pltpu.VMEM((2,) + block, jnp.bfloat16),
+            pltpu.VMEM((6,) + block, low),
+            pltpu.VMEM((7,) + block, low),
+            pltpu.VMEM((6,) + block, low),
+            pltpu.VMEM((12,) + block, low),
+            pltpu.VMEM((2,) + block, low),
             dma((7,)),
             dma((2,)),
             dma((10,)),
@@ -458,18 +521,19 @@
             dma((6,)),
             dma((2,)),
             dma((12,)),
+            dma((4 * kv_heads,)),
+            dma((4 * kv_heads,)),
         ],
         compiler_params=pltpu.CompilerParams(
             vmem_limit_bytes=60 * 2**20, collective_id=0, has_side_effects=True
         ),
         name="attention_backward",
-    )(lo, pos, local)
-    back = back.reshape(rows, 1, (group + 2) * dim)
-    back = lax.all_to_all(back, "head", split_axis=0, concat_axis=1, tiled=True)
+    )(doc_lengths, kv, qg)
+    by_token = lambda part: jnp.transpose(part, (1, 0, 2))
     return (
-        back[:, :, : group * dim].reshape(queries.shape),
-        back[:, :, group * dim : (group + 1) * dim],
-        back[:, :, (group + 1) * dim :],
+        by_token(dq).reshape(queries.shape),
+        by_token(dkv[:, :, :dim]),
+        by_token(dkv[:, :, dim:]),
     )
 
 

time: 128 us -> 107 us (0.84)
  Pallas kernels: 65.9 us -> 99.2 us
  blocking collectives: 22.7 us -> 0 us
  waiting for transfers between devices: 16.9 us -> 0 us
  starting transfers between devices: 11.6 us -> 0 us
  other arithmetic: 3.03 us -> 1.47 us
    pallas_call x1, Pallas kernels: 65.9 us -> 99.2 us  [body(): pl.pallas_call(attention_kernel, out_shape=(jax.ShapeDtypeStruct(swapped,...]
    all_to_all x1 -> x0, blocking collectives: 22.7 us -> none  [body(): back = lax.all_to_all(back, 'head', split_axis=0, concat_axis=1, tiled=True)]
    all_to_all x1 -> x0, waiting for transfers between devices: 16.9 us -> none  [body(): lax.all_to_all(packed, 'head', split_axis=1, concat_axis=0, tiled=True)]
    all_to_all x1 -> x0, starting transfers between devices: 11.6 us -> none  [body(): lax.all_to_all(packed, 'head', split_axis=1, concat_axis=0, tiled=True)]
    reshape x1 -> x0, other arithmetic: 1.89 us -> none  [body(): back = back.reshape(rows, 1, (group + 2) * dim)]
    reshape x6 -> x5, local copies, waits for them, and re-layouts: 2.5 us -> 1.01 us  [the longest x1 0.74 us: body(): by_token(dq).reshape(queries.shape)]
    transpose x0 -> x2, other arithmetic: none -> 1.47 us  [body(): jnp.transpose(jnp.concatenate([part.reshape(chunk, kv_heads, -1) for part...]
    unnamed x21 -> x12, local copies, waits for them, and re-layouts: 3.94 us -> 3.61 us
  transfers between devices with their start and end apart: 1 -> 0, of which waited for: 1 -> 0; matrix products, arithmetic and copies ran while one was open for 1% -> 0% of each run, Pallas kernels for 0% -> 0%
where the time goes in v2:
time: 107 us
  Pallas kernels  99.2 us (93%)
  local copies, waits for them, and re-layouts  5.62 us (5%)
  other arithmetic  1.47 us (1%)
    pallas_call x1, Pallas kernels, body(): pl.pallas_call(attention_kernel, out_shape=(jax.ShapeDtypeStruct(swapped,...  99.2 us
    unnamed x12, local copies, waits for them, and re-layouts  3.61 us

profile of v2, /device:TPU:6, one launch (start us, length us, event | category | flops | bytes accessed | tf_op | source)
XLA Modules:
  0.0 107.0 jit_solution(6404851307733116985)
XLA Ops:
  0.6 0.0 copy-start.3
  0.6 1.0 copy.12
  1.6 0.0 copy-done.3
  1.6 0.0 copy-start
  1.7 0.7 maximum_bitcast_fusion.1.kv_out_ref
  2.4 0.3 copy-done
  2.6 0.1 reshape.15
  2.7 0.0 copy-start.1
  2.7 0.1 copy.14
  2.8 0.8 copy-done.1
  3.6 0.1 reshape.16
  3.7 0.1 copy.15
  3.8 0.8 maximum_bitcast_fusion.qg_out_ref
  4.6 99.2 %attention_backward.1 = (bf16[16,24,256]{2,1,0:T(8,128)(2,1)}, bf16[16,24,256]{2,1,0:T(8,128)(2,1)}) custom-call(s32[8]{0:T(128)} %lengths_ref.1, bf16[16,24,256]{2,1,0:T(8,128)(2,1)} %maximum_bitcast_fusion.1.kv_out_ref, bf16[16,24,512]{2,1,0:T(8,128)(2,1)} %maximum_bitcast_fusion.qg_out_ref), custom_call_target="tpu_custom_call" | custom-call | tf_op jit(solution)/shard_map/attention_backward/pallas_call | solution.py:493
  103.7 1.0 copy.16
  104.7 0.0 copy-start.2
  104.7 0.7 reshape.17
  105.5 0.2 copy-done.2
  105.7 0.7 copy.18
  106.3 0.7 copy.17
  (2 shorter events, 0.1 us)
Async XLA Ops:
  0.6 1.0 copy-start.3
  1.6 1.0 copy-start
  2.7 0.9 copy-start.1
  104.7 0.9 copy-start.2

commit v3 on v2

--- a/solution.py
+++ b/solution.py
@@ -16,7 +16,7 @@
 
 def attention_kernel(
     lengths_ref, kv_out_ref, qg_out_ref, dq_back_ref, dkv_back_ref,
-    kv_in_ref, qg_in_ref, dq_out_ref, dkv_out_ref, kv_ref, s_ref, dp_ref, dq_ref, odd_ref, even_ref, pair_ref, got_ref, row_ref,
+    kv_in_ref, qg_in_ref, dq_out_ref, dkv_out_ref, kv_ref, s_ref, dp_ref, top_ref, sum_ref, dq_ref, odd_ref, even_ref, pair_ref, got_ref, row_ref,
     partner_send, across_send, chip_send, slot_recv, odd_send, even_send, pair_recv, row_send, got_recv,
     swap_send, swap_recv,
 ):
@@ -181,13 +181,13 @@
     lax.fori_loop(1, heads, greet_head, 0)
     pl.semaphore_wait(barrier, 5 + heads)
     swap_start(0, kv_out_ref, kv_in_ref)
-    swap_start(1, qg_out_ref, qg_in_ref)
     swap_arrived(0, kv_out_ref, kv_in_ref)
     kv_ref[0] = kv_in_ref[...].astype(jnp.float32).reshape(rows, 2 * dim).astype(jnp.bfloat16)
 
     to_next(start)
     along_own(start)
     to_partner(0, start)
+    swap_start(1, qg_out_ref, qg_in_ref)
 
     pos = my * rows + lax.broadcasted_iota(jnp.int32, (1, rows), 1)
     end = lengths_ref[0]
@@ -203,18 +203,27 @@
     q = jnp.concatenate([qg[:, :dim], qg[:, dim : 2 * dim]], axis=0)
     g = jnp.concatenate([qg[:, 2 * dim : 3 * dim], qg[:, 3 * dim :]], axis=0)
 
-    def scores(d, top):
+    def scores(d, state):
+        top, total, delta = state
         contract = (((1,), (1,)), ((), ()))
         s = lax.dot_general(kv_ref[d, :, :dim], q, contract, preferred_element_type=jnp.float32)
-        dp_ref[d] = lax.dot_general(
-            kv_ref[d, :, dim:], g, contract, preferred_element_type=jnp.float32
-        )
+        dp = lax.dot_general(kv_ref[d, :, dim:], g, contract, preferred_element_type=jnp.float32)
         k_pos = (my - d) * rows + lax.broadcasted_iota(jnp.int32, (rows, wide), 0)
         s = jnp.where((k_pos >= lo) & (k_pos <= pos), s, masked_value)
-        s_ref[d] = s
-        return jnp.maximum(top, jnp.max(s, axis=0, keepdims=True))
-
-    top = scores(0, jnp.full((1, wide), masked_value, jnp.float32))
+        new = jnp.maximum(top, jnp.max(s, axis=0, keepdims=True) * exp2_scale)
+        p = jnp.exp2(s * exp2_scale - new)
+        factor = jnp.exp2(top - new)
+        s_ref[d] = p
+        dp_ref[d] = dp
+        top_ref[d] = new
+        return (
+            new,
+            total * factor + jnp.sum(p, axis=0, keepdims=True),
+            delta * factor + jnp.sum(p * dp, axis=0, keepdims=True),
+        )
+
+    zero = jnp.zeros((1, wide), jnp.float32)
+    state = scores(0, (zero + masked_value, zero, zero))
 
     @pl.when(row >= 1)
     def _():
@@ -223,23 +232,23 @@
     to_second(start)
     along_first(start)
 
-    def even_step(j, top):
+    def even_step(j, state):
         @pl.when(j != 4)
         def _():
             arrived(2 * j)
 
         to_partner(j, start)
-        return scores(2 * j, top)
+        return scores(2 * j, state)
 
     even_end = jnp.minimum(order, 5) + 1
-    top = lax.fori_loop(1, jnp.minimum(even_end, 3), even_step, top)
+    state = lax.fori_loop(1, jnp.minimum(even_end, 3), even_step, state)
 
     @pl.when((row >= 2) & relays)
     def _():
         arrived(extra)
 
     along_second(start)
-    top = lax.fori_loop(3, even_end, even_step, top)
+    state = lax.fori_loop(3, even_end, even_step, state)
     last = (core == 1) & (order >= 6)
 
     @pl.when(last)
@@ -247,36 +256,20 @@
         arrived(12)
         slot_copy(12, 11, partner_send.at[6], place(row, chip, 0)).start()
 
-    def odd_step(j, top):
+    def odd_step(j, state):
         arrived(2 * j + 1)
-        return scores(2 * j + 1, top)
-
-    top = lax.fori_loop(0, jnp.minimum(order + core, 6), odd_step, top)
-    top = top * exp2_scale
-
-    def second(d, state):
-        total, delta = state
-        p = jnp.exp2(s_ref[d] * exp2_scale - top)
-        s_ref[d] = p
-        return (
-            total + jnp.sum(p, axis=0, keepdims=True),
-            delta + jnp.sum(p * dp_ref[d], axis=0, keepdims=True),
-        )
-
-    zero = jnp.zeros((1, wide), jnp.float32)
-    total, delta = lax.fori_loop(0, jnp.minimum(my + 1, reach), second, (zero, zero))
+        return scores(2 * j + 1, state)
+
+    top, total, delta = lax.fori_loop(0, jnp.minimum(order + core, 6), odd_step, state)
     inverse = 1.0 / total
     delta = delta * inverse
-    column = jnp.transpose(jnp.broadcast_to(inverse, (dim, wide)))
-    g_low = (g.astype(jnp.float32) * column).astype(jnp.bfloat16)
-    q_low = (q.astype(jnp.float32) * (column * score_scale)).astype(jnp.bfloat16)
     dq_ref[...] = jnp.zeros_like(dq_ref)
 
     def gradients(d):
-        p = s_ref[d]
+        p = s_ref[d] * (jnp.exp2(top_ref[d] - top) * inverse)
         ds = (p * (dp_ref[d] - delta)).astype(jnp.bfloat16)
-        dv = jnp.dot(p.astype(jnp.bfloat16), g_low, preferred_element_type=jnp.float32)
-        dk = jnp.dot(ds, q_low, preferred_element_type=jnp.float32)
+        dv = jnp.dot(p.astype(jnp.bfloat16), g, preferred_element_type=jnp.float32)
+        dk = jnp.dot(ds, q, preferred_element_type=jnp.float32) * score_scale
         dq_ref[...] += lax.dot_general(
             kv_ref[d, :, :dim], ds, (((0,), (0,)), ((), ())), preferred_element_type=jnp.float32
         )
@@ -360,22 +353,9 @@
 
         return carry
 
-    lax.fori_loop(0, jnp.minimum(order, 5) + 1, third, 0)
-
-    @pl.when(core == 1)
-    def _():
-        dk, dv = gradients(0)
-        even_ref[0, :, :dim] = dk.astype(jnp.bfloat16)
-        even_ref[0, :, dim:] = dv.astype(jnp.bfloat16)
-
-    dq = jnp.transpose(dq_ref[...] * (inverse * score_scale))
-    for part in range(2):
-        dq_out_ref[:, :, part * dim : (part + 1) * dim] = (
-            dq[part * rows : (part + 1) * rows].reshape(heads, chunk, dim).astype(jnp.bfloat16)
-        )
-    swap_start(2, dq_out_ref, dq_back_ref)
-
-    acc = dp_ref.at[0, :, : 2 * dim]
+    lax.fori_loop(0, jnp.minimum(even_end, 3), third, 0)
+
+    acc = sum_ref
 
     def add(index):
         got(index)
@@ -400,6 +380,21 @@
 
         row_ref[1] = acc[...].astype(jnp.bfloat16)
         row_copy(1).start()
+
+    lax.fori_loop(3, even_end, third, 0)
+
+    @pl.when(core == 1)
+    def _():
+        dk, dv = gradients(0)
+        even_ref[0, :, :dim] = dk.astype(jnp.bfloat16)
+        even_ref[0, :, dim:] = dv.astype(jnp.bfloat16)
+
+    dq = jnp.transpose(dq_ref[...] * score_scale)
+    for part in range(2):
+        dq_out_ref[:, :, part * dim : (part + 1) * dim] = (
+            dq[part * rows : (part + 1) * rows].reshape(heads, chunk, dim).astype(jnp.bfloat16)
+        )
+    swap_start(2, dq_out_ref, dq_back_ref)
 
     @pl.when(row >= 1)
     def _():
@@ -506,6 +501,8 @@
             pltpu.VMEM((14,) + block, low),
             pltpu.VMEM((reach, rows, wide), jnp.float32),
             pltpu.VMEM((reach, rows, wide), jnp.float32),
+            pltpu.VMEM((reach, 1, wide), jnp.float32),
+            pltpu.VMEM(block, jnp.float32),
             pltpu.VMEM((dim, wide), jnp.float32),
             pltpu.VMEM((6,) + block, low),
             pltpu.VMEM((7,) + block, low),

time: 107 us -> 106 us (level)
  Pallas kernels: 99.2 us -> 97.9 us
    pallas_call x1, Pallas kernels: 99.2 us -> 97.9 us  [body(): pl.pallas_call(attention_kernel, out_shape=(jax.ShapeDtypeStruct(swapped,...]
where the time goes in v3:
time: 106 us
  Pallas kernels  97.9 us (92%)
  local copies, waits for them, and re-layouts  5.62 us (5%)
  other arithmetic  1.47 us (1%)
    pallas_call x1, Pallas kernels, body(): pl.pallas_call(attention_kernel, out_shape=(jax.ShapeDtypeStruct(swapped,...  97.9 us
    unnamed x12, local copies, waits for them, and re-layouts  3.61 us

profile of v3, /device:TPU:6, one launch (start us, length us, event | category | flops | bytes accessed | tf_op | source)
XLA Modules:
  0.0 105.7 jit_solution(15785311491505830904)
XLA Ops:
  0.6 0.0 copy-start.3
  0.6 1.0 copy.12
  1.6 0.0 copy-done.3
  1.6 0.0 copy-start
  1.7 0.7 maximum_bitcast_fusion.1.kv_out_ref
  2.4 0.3 copy-done
  2.6 0.1 reshape.15
  2.7 0.0 copy-start.1
  2.7 0.1 copy.14
  2.8 0.8 copy-done.1
  3.6 0.1 reshape.16
  3.7 0.1 copy.15
  3.8 0.8 maximum_bitcast_fusion.qg_out_ref
  4.6 97.9 %attention_backward.1 = (bf16[16,24,256]{2,1,0:T(8,128)(2,1)}, bf16[16,24,256]{2,1,0:T(8,128)(2,1)}) custom-call(s32[8]{0:T(128)} %lengths_ref.1, bf16[16,24,256]{2,1,0:T(8,128)(2,1)} %maximum_bitcast_fusion.1.kv_out_ref, bf16[16,24,512]{2,1,0:T(8,128)(2,1)} %maximum_bitcast_fusion.qg_out_ref), custom_call_target="tpu_custom_call" | custom-call | tf_op jit(solution)/shard_map/attention_backward/pallas_call | solution.py:488
  102.4 1.0 copy.16
  103.4 0.0 copy-start.2
  103.4 0.7 reshape.17
  104.1 0.2 copy-done.2
  104.4 0.7 copy.18
  105.0 0.7 copy.17
  (2 shorter events, 0.1 us)
Async XLA Ops:
  0.6 1.0 copy-start.3
  1.6 1.0 copy-start
  2.7 0.9 copy-start.1
  103.4 0.9 copy-start.2

commit v4 on v3

--- a/solution.py
+++ b/solution.py
@@ -15,15 +15,14 @@
 
 
 def attention_kernel(
-    lengths_ref, kv_out_ref, qg_out_ref, dq_back_ref, dkv_back_ref,
-    kv_in_ref, qg_in_ref, dq_out_ref, dkv_out_ref, kv_ref, s_ref, dp_ref, top_ref, sum_ref, dq_ref, odd_ref, even_ref, pair_ref, got_ref, row_ref,
+    lengths_ref, k_out_ref, v_out_ref, qg_out_ref, dq_back_ref, dkv_back_ref,
+    k_in_ref, v_in_ref, qg_in_ref, dq_out_ref, dkv_out_ref, kv_ref, s_ref, dp_ref, top_ref, sum_ref, dq_ref, odd_ref, even_ref, pair_ref, got_ref, row_ref,
     partner_send, across_send, chip_send, slot_recv, odd_send, even_send, pair_recv, row_send, got_recv,
     swap_send, swap_recv,
 ):
-    heads, chunk, _ = kv_out_ref.shape
+    heads, chunk, dim = k_out_ref.shape
     rows = heads * chunk
     reach, _, wide = s_ref.shape
-    dim = kv_ref.shape[2] // 2
     my = lax.axis_index("seq")
     my_head = lax.axis_index("head")
     grid_rows = lax.axis_size("seq") // 8
@@ -45,11 +44,17 @@
             device_id_type=pl.DeviceIdType.MESH,
         )
 
-    def slot_copy(source, target, send, device):
-        return remote(kv_ref.at[source], kv_ref.at[target], send, slot_recv.at[target], device)
-
-    def arrived(slot):
-        slot_copy(slot, slot, chip_send.at[0], place(row, chip, core)).wait_recv()
+    def slot_copy(half, source, target, sends, index, device):
+        return remote(
+            kv_ref.at[half, source],
+            kv_ref.at[half, target],
+            sends.at[2 * index + half],
+            slot_recv.at[2 * target + half],
+            device,
+        )
+
+    def arrived(half, slot):
+        slot_copy(half, slot, slot, chip_send, 0, place(row, chip, core)).wait_recv()
 
     def got(index):
         remote(
@@ -64,57 +69,47 @@
     has_next = row < grid_rows - 1
     relays = chip >= 3 - core
 
-    def to_next(act):
+    def to_next(half, act):
         @pl.when(has_next)
         def _():
-            act(slot_copy(0, 8, across_send.at[0], place(row + 1, chip, core)))
-
-    def to_second(act):
+            act(slot_copy(half, 0, 8, across_send, 0, place(row + 1, chip, core)))
+
+    def to_second(half, act):
         @pl.when((row >= 1) & has_next & relays)
         def _():
-            act(slot_copy(8, extra, across_send.at[1], place(row + 1, chip, core)))
-
-    def along_own(act):
+            act(slot_copy(half, 8, extra, across_send, 1, place(row + 1, chip, core)))
+
+    def along_own(half, act):
         for other in range(4):
             @pl.when(chip < other)
             def _(other=other):
-                act(
-                    slot_copy(
-                        0, 2 * (other - chip), chip_send.at[other], place(row, other, core)
-                    )
-                )
-
-    def along_first(act):
+                target = 2 * (other - chip)
+                act(slot_copy(half, 0, target, chip_send, other, place(row, other, core)))
+
+    def along_first(half, act):
         for other in range(4):
             @pl.when((row >= 1) & (chip != other) & (chip + 1 + core >= other))
             def _(other=other):
-                act(
-                    slot_copy(
-                        8, 8 + 2 * (other - chip), chip_send.at[4 + other], place(row, other, core)
-                    )
-                )
-
-    def along_second(act):
+                target = 8 + 2 * (other - chip)
+                act(slot_copy(half, 8, target, chip_send, 4 + other, place(row, other, core)))
+
+    def along_second(half, act):
         for other in range(2):
             @pl.when((row >= 2) & (chip - 3 + core >= other))
             def _(other=other):
+                target = 16 + 2 * (other - chip)
                 act(
-                    slot_copy(
-                        extra,
-                        16 + 2 * (other - chip),
-                        chip_send.at[8 + other],
-                        place(row, other, core),
-                    )
+                    slot_copy(half, extra, target, chip_send, 8 + other, place(row, other, core))
                 )
 
-    def to_partner(j, act):
+    def to_partner(half, j, act):
         @pl.when(core == 0)
         def _():
-            act(slot_copy(2 * j, 2 * j + 1, partner_send.at[j], place(row, chip, 1)))
+            act(slot_copy(half, 2 * j, 2 * j + 1, partner_send, j, place(row, chip, 1)))
 
         @pl.when((core == 1) & (j >= 1))
         def _():
-            act(slot_copy(2 * j, 2 * j - 1, partner_send.at[j], place(row, chip, 0)))
+            act(slot_copy(half, 2 * j, 2 * j - 1, partner_send, j, place(row, chip, 0)))
 
     def start(copy):
         copy.start()
@@ -180,14 +175,27 @@
 
     lax.fori_loop(1, heads, greet_head, 0)
     pl.semaphore_wait(barrier, 5 + heads)
-    swap_start(0, kv_out_ref, kv_in_ref)
-    swap_arrived(0, kv_out_ref, kv_in_ref)
-    kv_ref[0] = kv_in_ref[...].astype(jnp.float32).reshape(rows, 2 * dim).astype(jnp.bfloat16)
-
-    to_next(start)
-    along_own(start)
-    to_partner(0, start)
+    swap_start(0, k_out_ref, k_in_ref)
+    swap_sent(0, k_out_ref, k_in_ref)
+    swap_start(4, v_out_ref, v_in_ref)
+
+    def begin(half, n, source, target):
+        swap_arrived(n, source, target)
+        kv_ref[half, 0] = target[...].astype(jnp.float32).reshape(rows, dim).astype(jnp.bfloat16)
+        to_next(half, start)
+        along_own(half, start)
+        to_partner(half, 0, start)
+
+    begin(0, 0, k_out_ref, k_in_ref)
+    begin(1, 4, v_out_ref, v_in_ref)
     swap_start(1, qg_out_ref, qg_in_ref)
+    for half in range(2):
+        @pl.when(row >= 1)
+        def _(half=half):
+            arrived(half, 8)
+
+        to_second(half, start)
+        along_first(half, start)
 
     pos = my * rows + lax.broadcasted_iota(jnp.int32, (1, rows), 1)
     end = lengths_ref[0]
@@ -206,8 +214,8 @@
     def scores(d, state):
         top, total, delta = state
         contract = (((1,), (1,)), ((), ()))
-        s = lax.dot_general(kv_ref[d, :, :dim], q, contract, preferred_element_type=jnp.float32)
-        dp = lax.dot_general(kv_ref[d, :, dim:], g, contract, preferred_element_type=jnp.float32)
+        s = lax.dot_general(kv_ref[0, d], q, contract, preferred_element_type=jnp.float32)
+        dp = lax.dot_general(kv_ref[1, d], g, contract, preferred_element_type=jnp.float32)
         k_pos = (my - d) * rows + lax.broadcasted_iota(jnp.int32, (rows, wide), 0)
         s = jnp.where((k_pos >= lo) & (k_pos <= pos), s, masked_value)
         new = jnp.maximum(top, jnp.max(s, axis=0, keepdims=True) * exp2_scale)
@@ -225,39 +233,38 @@
     zero = jnp.zeros((1, wide), jnp.float32)
     state = scores(0, (zero + masked_value, zero, zero))
 
-    @pl.when(row >= 1)
-    def _():
-        arrived(8)
-
-    to_second(start)
-    along_first(start)
-
     def even_step(j, state):
-        @pl.when(j != 4)
-        def _():
-            arrived(2 * j)
-
-        to_partner(j, start)
+        for half in range(2):
+            @pl.when(j != 4)
+            def _(half=half):
+                arrived(half, 2 * j)
+
+            to_partner(half, j, start)
+
         return scores(2 * j, state)
 
     even_end = jnp.minimum(order, 5) + 1
     state = lax.fori_loop(1, jnp.minimum(even_end, 3), even_step, state)
 
-    @pl.when((row >= 2) & relays)
-    def _():
-        arrived(extra)
-
-    along_second(start)
+    for half in range(2):
+        @pl.when((row >= 2) & relays)
+        def _(half=half):
+            arrived(half, extra)
+
+        along_second(half, start)
+
     state = lax.fori_loop(3, even_end, even_step, state)
     last = (core == 1) & (order >= 6)
 
     @pl.when(last)
     def _():
-        arrived(12)
-        slot_copy(12, 11, partner_send.at[6], place(row, chip, 0)).start()
+        for half in range(2):
+            arrived(half, 12)
+            slot_copy(half, 12, 11, partner_send, 6, place(row, chip, 0)).start()
 
     def odd_step(j, state):
-        arrived(2 * j + 1)
+        arrived(0, 2 * j + 1)
+        arrived(1, 2 * j + 1)
         return scores(2 * j + 1, state)
 
     top, total, delta = lax.fori_loop(0, jnp.minimum(order + core, 6), odd_step, state)
@@ -271,7 +278,7 @@
         dv = jnp.dot(p.astype(jnp.bfloat16), g, preferred_element_type=jnp.float32)
         dk = jnp.dot(ds, q, preferred_element_type=jnp.float32) * score_scale
         dq_ref[...] += lax.dot_general(
-            kv_ref[d, :, :dim], ds, (((0,), (0,)), ((), ())), preferred_element_type=jnp.float32
+            kv_ref[0, d], ds, (((0,), (0,)), ((), ())), preferred_element_type=jnp.float32
         )
         return dk, dv
 
@@ -424,21 +431,24 @@
     dkv_out_ref[...] = acc[...].reshape(heads, chunk, 2 * dim).astype(jnp.bfloat16)
     swap_start(3, dkv_out_ref, dkv_back_ref)
 
-    to_next(sent)
-    along_own(sent)
-    to_second(sent)
-    along_first(sent)
-    along_second(sent)
+    for half in range(2):
+        to_next(half, sent)
+        along_own(half, sent)
+        to_second(half, sent)
+        along_first(half, sent)
+        along_second(half, sent)
 
     def sent_pair(j, carry):
-        to_partner(j, sent)
+        to_partner(0, j, sent)
+        to_partner(1, j, sent)
         return carry
 
     lax.fori_loop(0, even_end, sent_pair, 0)
 
     @pl.when(last)
     def _():
-        slot_copy(12, 11, partner_send.at[6], place(row, chip, 0)).wait_send()
+        for half in range(2):
+            slot_copy(half, 12, 11, partner_send, 6, place(row, chip, 0)).wait_send()
 
     def sent_gradients(j, carry):
         @pl.when((core == 1) | (j < order))
@@ -461,7 +471,7 @@
     def _():
         row_copy(0).wait_send()
 
-    swap_sent(0, kv_out_ref, kv_in_ref)
+    swap_sent(4, v_out_ref, v_in_ref)
     swap_sent(1, qg_out_ref, qg_in_ref)
     swap_sent(2, dq_out_ref, dq_back_ref)
     swap_sent(3, dkv_out_ref, dkv_back_ref)
@@ -476,7 +486,8 @@
     by_head = lambda parts: jnp.transpose(
         jnp.concatenate([part.reshape(chunk, kv_heads, -1) for part in parts], axis=2), (1, 0, 2)
     )
-    kv = by_head([keys, values])
+    k = by_head([keys])
+    v = by_head([values])
     qg = by_head([queries, output_gradient])
     reach = (WINDOW - 1) // rows + 2
     wide = group * rows
@@ -491,14 +502,15 @@
             jax.ShapeDtypeStruct(swapped, low),
             jax.ShapeDtypeStruct(swapped, low),
         ),
-        in_specs=[pl.BlockSpec(memory_space=pltpu.SMEM), vmem, vmem],
+        in_specs=[pl.BlockSpec(memory_space=pltpu.SMEM), vmem, vmem, vmem],
         out_specs=(vmem, vmem),
         scratch_shapes=[
-            pltpu.VMEM(swapped, low),
+            pltpu.VMEM((kv_heads, chunk, dim), low),
+            pltpu.VMEM((kv_heads, chunk, dim), low),
             pltpu.VMEM((kv_heads, chunk, 4 * dim), low),
             pltpu.VMEM(swapped, low),
             pltpu.VMEM(swapped, low),
-            pltpu.VMEM((14,) + block, low),
+            pltpu.VMEM((2, 14, rows, dim), low),
             pltpu.VMEM((reach, rows, wide), jnp.float32),
             pltpu.VMEM((reach, rows, wide), jnp.float32),
             pltpu.VMEM((reach, 1, wide), jnp.float32),
@@ -509,23 +521,23 @@
             pltpu.VMEM((6,) + block, low),
             pltpu.VMEM((12,) + block, low),
             pltpu.VMEM((2,) + block, low),
-            dma((7,)),
-            dma((2,)),
-            dma((10,)),
             dma((14,)),
+            dma((4,)),
+            dma((20,)),
+            dma((28,)),
             dma((6,)),
             dma((7,)),
             dma((6,)),
             dma((2,)),
             dma((12,)),
-            dma((4 * kv_heads,)),
-            dma((4 * kv_heads,)),
+            dma((5 * kv_heads,)),
+            dma((5 * kv_heads,)),
         ],
         compiler_params=pltpu.CompilerParams(
             vmem_limit_bytes=60 * 2**20, collective_id=0, has_side_effects=True
         ),
         name="attention_backward",
-    )(doc_lengths, kv, qg)
+    )(doc_lengths, k, v, qg)
     by_token = lambda part: jnp.transpose(part, (1, 0, 2))
     return (
         by_token(dq).reshape(queries.shape),

time: 106 us -> 101 us (0.953)
  the two profiles are of different devices: /device:TPU:6 before, /device:TPU:22 now
where the time goes in v4:
time: 101 us
  Pallas kernels  92.9 us (92%)
  local copies, waits for them, and re-layouts  6.2 us (6%)
    pallas_call x1, Pallas kernels, body(): pl.pallas_call(attention_kernel, out_shape=(jax.ShapeDtypeStruct(swapped,...  92.9 us
    unnamed x10, local copies, waits for them, and re-layouts  2.55 us

profile of v4, /device:TPU:22, one launch (start us, length us, event | category | flops | bytes accessed | tf_op | source)
XLA Modules:
  0.0 100.6 jit_solution(9961551881498678781)
XLA Ops:
  0.6 1.0 reshape.15
  1.6 0.0 copy-start
  1.6 0.1 copy.14
  1.7 0.8 copy-done
  2.6 0.1 reshape.16
  2.6 0.1 copy.15
  2.7 0.0 copy-start.2
  2.7 0.0 copy-start.3
  2.7 0.8 maximum_bitcast_fusion.qg_out_ref
  3.5 0.1 copy-done.2
  3.6 0.1 copy-done.3
  3.7 0.7 copy_bitcast_fusion
  4.4 92.9 %attention_backward.1 = (bf16[16,24,256]{2,1,0:T(8,128)(2,1)}, bf16[16,24,256]{2,1,0:T(8,128)(2,1)}) custom-call(s32[8]{0:T(128)} %lengths_ref.1, bf16[16,24,128]{2,1,0:T(8,128)(2,1)} %get-tuple-element.16.k_out_ref, bf16[16,24,128]{2,1,0:T(8,128)(2,1)} %get-tuple-element.15.v_out_ref, bf16[16,24,512]{2,1,0:T(8,128)(2,1)} %maximum_bitcast_fusion.qg_out_ref), custom_call_target="tpu_custom_call" | custom-call | tf_op jit(solution)/shard_map/attention_backward/pallas_call | solution.py:499
  97.4 1.0 copy.16
  98.4 0.0 copy-start.1
  98.4 0.7 reshape.17
  99.1 0.2 copy-done.1
  99.3 0.7 copy.18
  100.0 0.7 copy.17
  (1 shorter events, 0.0 us)
Async XLA Ops:
  1.6 0.9 copy-start
  2.7 0.9 copy-start.2
  2.7 1.0 copy-start.3
  98.4 0.9 copy-start.1
